TPU v7x, 512 devices: a whole 4x4x16 slice. The times are simulated.
512 devices in a mesh: blk: 16 (over y_hi, x, core), dom: 32 (over y_lo, z).
Axes of the slice: x: 4, y: 4 (y_hi: 2, y_lo: 2; y = y_hi * 2 + y_lo), z: 16, core: 2. Of those that a mesh axis runs over, the one named last changes fastest.
Arguments:
- nodes: bfloat16 [65536, 512], P(('blk', 'dom')), may hold values from -6 to 6
- experts_list: int32 [512, 4], P(('blk', 'dom')), may hold values from 0 to 15, all different within a row
- w_query: bfloat16 [512, 512], replicated
- w_key: bfloat16 [512, 512], replicated
- w_value: bfloat16 [512, 512], replicated, may hold values from -0.25 to 0.25
- w_out: bfloat16 [512, 512], replicated, may hold values from -0.25 to 0.25
- w_up: bfloat16 [512, 1024], replicated, may hold values from -0.25 to 0.25
- w_down: bfloat16 [1024, 512], replicated, may hold values from -0.1875 to 0.1875
- cotangent: bfloat16 [65536, 512], P(('blk', 'dom')), may hold values from -6 to 6
Outputs:
- layer_out: bfloat16 [65536, 512], P(('blk', 'dom'))
- grad_nodes: bfloat16 [65536, 512], P(('blk', 'dom'))
Inputs may be any that keep to these rules, and one draw needn't show every extreme that they name: `experts_list`: row g names 4 different values; value c stands for the block held at blk index c and the same dom index as block g. Every value is named by some row.
All inputs are finite; a program needn't handle non-finite values.
Results may differ from a plain program's by a relative error of at most 0.0057.
Values may be sent and summed in bfloat16 or wider, within the bound.
A program may use at most 128 MiB of HBM per device.

v0:
```python
import jax
import jax.numpy as jnp
from jax import lax
from jax.sharding import PartitionSpec as P

H = 8
HEAD = 64
EPS = 1e-05
NEG = -1e30


def with_halo(array, sides, width):
    for axis, dim in sides:
        devices, length = (lax.axis_size(axis), array.shape[dim])
        up = [(i, (i + 1) % devices) for i in range(devices)]
        down = [(j, i) for i, j in up]
        last = lax.slice_in_dim(array, length - width, length, axis=dim)
        leading = lax.slice_in_dim(array, 0, width, axis=dim)
        before = lax.ppermute(last, axis, up)
        after = lax.ppermute(leading, axis, down)
        array = jnp.concatenate([before, array, after], axis=dim)
    return array


def shifted(array, axis, by):
    devices = lax.axis_size(axis)
    return lax.ppermute(array, axis, [(i, (i + by) % devices) for i in range(devices)])


def normalize(values):
    mean_v = jnp.mean(values, axis=-1, keepdims=True)
    centered = values - mean_v
    inv_std = lax.rsqrt(jnp.mean(centered * centered, axis=-1, keepdims=True) + EPS)
    return (centered * inv_std, inv_std)


def normalize_back(values, upstream):
    unit, inv_std = normalize(values)
    return inv_std * (
        upstream
        - jnp.mean(upstream, axis=-1, keepdims=True)
        - unit * jnp.mean(upstream * unit, axis=-1, keepdims=True)
    )


def heads_of(rows):
    return rows.reshape(rows.shape[0], H, HEAD)


def attend(queries, keyvals):
    width = queries.shape[1]
    scale = HEAD ** (-0.5)
    qh = heads_of(queries)
    kh = heads_of(keyvals[:, :width])
    vh = heads_of(keyvals[:, width:])
    scores = jnp.einsum("qhd,khd->hqk", qh, kh, preferred_element_type=jnp.float32) * scale
    top = jnp.max(scores, axis=-1, keepdims=True)
    weights = jnp.exp(scores - top)
    total = jnp.sum(weights, axis=-1, keepdims=True)
    mixed = jnp.einsum(
        "hqk,khd->qhd", weights.astype(jnp.bfloat16), vh, preferred_element_type=jnp.float32
    )
    mixed = mixed / jnp.transpose(total, (1, 0, 2))
    lse = (top + jnp.log(total))[..., 0]
    return (mixed.reshape(queries.shape[0], width).astype(jnp.bfloat16), lse)


def attend_back(queries, keyvals, grad_out, lse, delta, qmult):
    width = queries.shape[1]
    scale = HEAD ** (-0.5)
    qh = heads_of(queries)
    kh = heads_of(keyvals[:, :width])
    vh = heads_of(keyvals[:, width:])
    gh = heads_of(grad_out)
    scores = jnp.einsum("qhd,khd->hqk", qh, kh, preferred_element_type=jnp.float32) * scale
    valid = qmult[None, :, None] > 0
    scores = jnp.where(valid, scores, NEG)
    probs = jnp.exp(scores - lse[..., None]) * qmult[None, :, None]
    grad_v = jnp.einsum(
        "hqk,qhd->khd", probs.astype(jnp.bfloat16), gh, preferred_element_type=jnp.float32
    )
    dprob = jnp.einsum("qhd,khd->hqk", gh, vh, preferred_element_type=jnp.float32)
    dscore = (probs * (dprob - delta[..., None]) * scale).astype(jnp.bfloat16)
    grad_q = jnp.einsum("hqk,khd->qhd", dscore, kh, preferred_element_type=jnp.float32)
    grad_k = jnp.einsum("hqk,qhd->khd", dscore, qh, preferred_element_type=jnp.float32)
    count = keyvals.shape[0]
    return (
        grad_q.reshape(queries.shape[0], width),
        jnp.concatenate([grad_k.reshape(count, width), grad_v.reshape(count, width)], 1),
    )


def on_device(nodes, experts_list, w_query, w_key, w_value, w_out, w_up, w_down, cotangent):
    f32 = jnp.float32
    bf16 = jnp.bfloat16
    rows, width = nodes.shape
    groups = lax.axis_size("blk")
    place = lax.axis_index("blk")
    x_full = nodes.astype(f32)
    unit, _ = normalize(x_full)
    normed = unit.astype(bf16)
    queries = jnp.dot(normed, w_query, preferred_element_type=f32).astype(bf16)
    keys = jnp.dot(normed, w_key, preferred_element_type=f32).astype(bf16)
    values = jnp.dot(normed, w_value, preferred_element_type=f32).astype(bf16)
    keyvals = jnp.concatenate([keys, values], 1)
    window = with_halo(keyvals, (("dom", 0),), rows)
    panels = lax.all_gather(keyvals, "blk", axis=0, tiled=True)
    listed = experts_list[0]
    listed_count = listed.shape[0]
    chosen = jnp.take(panels.reshape(groups, rows, 2 * width), listed, axis=0)
    all_keys = jnp.concatenate([window, chosen.reshape(listed_count * rows, 2 * width)], 0)
    mixed, lse = attend(queries, all_keys)
    resid = x_full + jnp.dot(mixed, w_out, preferred_element_type=f32)
    unit2, _ = normalize(resid)
    normed2 = unit2.astype(bf16)
    pre = jnp.dot(normed2, w_up, preferred_element_type=f32)
    act, gelu_back = jax.vjp(jax.nn.gelu, pre)
    layer_out = (resid + jnp.dot(act.astype(bf16), w_down, preferred_element_type=f32)).astype(bf16)
    grad_act = jnp.dot(cotangent, w_down.T, preferred_element_type=f32)
    grad_pre = gelu_back(grad_act)[0].astype(bf16)
    grad_norm2 = jnp.dot(grad_pre, w_up.T, preferred_element_type=f32)
    grad_resid = cotangent.astype(f32) + normalize_back(resid, grad_norm2)
    grad_mixed = jnp.dot(grad_resid.astype(bf16), w_out.T, preferred_element_type=f32).astype(bf16)
    delta = jnp.sum(heads_of(grad_mixed).astype(f32) * heads_of(mixed).astype(f32), axis=-1).T
    ones_rows = jnp.ones((rows,), f32)
    grad_q, grad_kv = attend_back(queries, all_keys, grad_mixed, lse, delta, ones_rows)
    from_upper = shifted(grad_kv[:rows].astype(jnp.bfloat16), "dom", -1).astype(jnp.float32)
    from_lower = shifted(grad_kv[2 * rows : 3 * rows].astype(jnp.bfloat16), "dom", 1).astype(
        jnp.float32
    )
    own_grad = grad_kv[rows : 2 * rows] + from_upper + from_lower
    listed_parts = grad_kv[3 * rows :].reshape(listed_count, rows, 2 * width)
    onehot = (listed[:, None] == jnp.arange(groups, dtype=jnp.int32)[None, :]).astype(f32)
    far_parts = jnp.einsum("eg,erc->grc", onehot, listed_parts).reshape(groups * rows, 2 * width)

    def carry_step(step, running):
        running = shifted(running.astype(jnp.bfloat16), "blk", 1).astype(running.dtype)
        target = (place - step - 1) % groups
        return running + lax.dynamic_slice_in_dim(far_parts, target * rows, rows, 0)

    first = lax.dynamic_slice_in_dim(far_parts, (place - 1) % groups * rows, rows, 0)
    far_grad = lax.fori_loop(1, groups, carry_step, first)
    key_grad = own_grad + far_grad
    grad_in = (
        jnp.dot(grad_q.astype(bf16), w_query.T, preferred_element_type=f32)
        + jnp.dot(key_grad[:, :width].astype(bf16), w_key.T, preferred_element_type=f32)
        + jnp.dot(key_grad[:, width:].astype(bf16), w_value.T, preferred_element_type=f32)
    )
    grad_nodes = (grad_resid + normalize_back(x_full, grad_in)).astype(bf16)
    return (layer_out, grad_nodes)


def solution(mesh):
    return jax.shard_map(
        on_device,
        mesh=mesh,
        in_specs=(
            P(("blk", "dom"), None),
            P(("blk", "dom"), None),
            P(),
            P(),
            P(),
            P(),
            P(),
            P(),
            P(("blk", "dom"), None),
        ),
        out_specs=(P(("blk", "dom"), None), P(("blk", "dom"), None)),
        check_vma=False,
    )
```

profile of v0, /device:TPU:8, one launch (start us, length us, event | category | flops | bytes accessed | tf_op | source)
XLA Modules:
  0.0 364.6 jit_solution(6669680879408683189)
XLA Ops:
  13.0 11.3 %collective-permute-start.2 = (bf16[128,1024]{1,0:T(8,128)(2,1)}, bf16[128,1024]{1,0:T(8,128)(2,1)S(1)}, u32[]{:S(2)}, u32[]{:S(2)}) collective-permute-start(bf16[128,1024]{1,0:T(8,128)(2,1)} %pad_maximum_fusion.2), channel_id=1, source_target_pairs={{1,0},{2,1},{3,2},{4,3},{5,4},{6,5},{7,6},{8,7},{9,8},{10,9},{11,1... | collective-permute-start | bytes 786440 | tf_op jit(solution)/shard_map/ppermute | solution.py:20
  24.3 1.9 collective-permute-start.1
  31.8 4.5 %collective-permute-done.1 = bf16[128,1024]{1,0:T(8,128)(2,1)S(1)} collective-permute-done((bf16[128,1024]{1,0:T(8,128)(2,1)}, bf16[128,1024]{1,0:T(8,128)(2,1)S(1)}, u32[]{:S(2)}, u32[]{:S(2)}) %collective-permute-start.1) | collective-permute-done | bytes 262176 | tf_op jit(solution)/shard_map/ppermute | solution.py:19
  37.1 51.1 %all-gather.2.cloned.1.call-done = bf16[2048,1024]{1,0:T(8,128)(2,1)} async-done(((bf16[128,1024]{1,0:T(8,128)(2,1)}), bf16[2048,1024]{1,0:T(8,128)(2,1)}) %all-gather.2.cloned.1.call-update) | async-done | bytes 4194320 | tf_op jit(solution)/shard_map/all_gather | solution.py:107
  88.2 2.8 gather_fusion
  99.1 3.6 fusion.82
  103.9 2.1 convolution_convert_fusion.1
  108.0 3.3 multiply_convert_fusion
  113.8 2.1 fusion.7
  117.7 2.8 copy.27
  126.2 4.9 %copy.29 = f32[16,128,1024]{2,1,0:T(8,128)S(1)} copy(f32[16,128,1024]{2,0,1:T(8,128)S(1)} %fusion.5) | data formatting | bytes 16777216 | tf_op jit(solution)/shard_map/eg,erc->grc/dot_general | solution.py:134
  131.1 2.8 fusion.83
  133.9 3.4 collective-permute-start.4
  137.3 5.3 %collective-permute-start.3 = (bf16[128,1024]{1,0:T(8,128)(2,1)}, bf16[128,1024]{1,0:T(8,128)(2,1)}, u32[]{:S(2)}, u32[]{:S(2)}) collective-permute-start(bf16[128,1024]{1,0:T(8,128)(2,1)} %get-tuple-element.127), channel_id=1, source_target_pairs={{0,31},{1,0},{2,1},{3,2},{4,3},{5,4},{6,5},{7,6},{8,7},{9,8},{10,9... | collective-permute-start | bytes 786440 | tf_op jit(solution)/shard_map/ppermute | solution.py:27
  142.7 211.9 %while.15 = (s32[]{:T(128)}, f32[128,1024]{1,0:T(8,128)S(1)}, s32[]{:T(128)}, f32[2048,1024]{1,0:T(8,128)}, s32[]{:T(128)}, /*index=5*/s32[]{:T(128)}, s32[]{:T(...) while((s32[]{:T(128)}, f32[128,1024]{1,0:T(8,128)S(1)}, s32[]{:T(128)}, f32[2048,1024]{1,0:T(8,128)}, ...), condition=%wide.region_10.11_spmd, body=%wide.region_9.10_spmd.sunk | while | flops 393235 | bytes 4194664 | solution.py:142
  143.4 1.9 collective-permute-start
  145.4 9.6 %collective-permute-done = bf16[128,1024]{1,0:T(8,128)(2,1)S(1)} collective-permute-done((bf16[128,1024]{1,0:T(8,128)(2,1)}, bf16[128,1024]{1,0:T(8,128)(2,1)S(1)}, u32[]{:S(2)}, u32[]{:S(2)}) %collective-permute-start) | collective-permute-done | bytes 262176 | tf_op jit(solution)/shard_map/while/body/eval_jaxpr/ppermute | solution.py:27
  157.6 1.9 collective-permute-start
  159.5 9.6 %collective-permute-done = bf16[128,1024]{1,0:T(8,128)(2,1)S(1)} collective-permute-done((bf16[128,1024]{1,0:T(8,128)(2,1)}, bf16[128,1024]{1,0:T(8,128)(2,1)S(1)}, u32[]{:S(2)}, u32[]{:S(2)}) %collective-permute-start) | collective-permute-done | bytes 262176 | tf_op jit(solution)/shard_map/while/body/eval_jaxpr/ppermute | solution.py:27
  173.6 9.6 %collective-permute-done = bf16[128,1024]{1,0:T(8,128)(2,1)S(1)} collective-permute-done((bf16[128,1024]{1,0:T(8,128)(2,1)}, bf16[128,1024]{1,0:T(8,128)(2,1)S(1)}, u32[]{:S(2)}, u32[]{:S(2)}) %collective-permute-start) | collective-permute-done | bytes 262176 | tf_op jit(solution)/shard_map/while/body/eval_jaxpr/ppermute | solution.py:27
  187.8 9.6 %collective-permute-done = bf16[128,1024]{1,0:T(8,128)(2,1)S(1)} collective-permute-done((bf16[128,1024]{1,0:T(8,128)(2,1)}, bf16[128,1024]{1,0:T(8,128)(2,1)S(1)}, u32[]{:S(2)}, u32[]{:S(2)}) %collective-permute-start) | collective-permute-done | bytes 262176 | tf_op jit(solution)/shard_map/while/body/eval_jaxpr/ppermute | solution.py:27
  201.9 9.6 %collective-permute-done = bf16[128,1024]{1,0:T(8,128)(2,1)S(1)} collective-permute-done((bf16[128,1024]{1,0:T(8,128)(2,1)}, bf16[128,1024]{1,0:T(8,128)(2,1)S(1)}, u32[]{:S(2)}, u32[]{:S(2)}) %collective-permute-start) | collective-permute-done | bytes 262176 | tf_op jit(solution)/shard_map/while/body/eval_jaxpr/ppermute | solution.py:27
  216.0 9.6 %collective-permute-done = bf16[128,1024]{1,0:T(8,128)(2,1)S(1)} collective-permute-done((bf16[128,1024]{1,0:T(8,128)(2,1)}, bf16[128,1024]{1,0:T(8,128)(2,1)S(1)}, u32[]{:S(2)}, u32[]{:S(2)}) %collective-permute-start) | collective-permute-done | bytes 262176 | tf_op jit(solution)/shard_map/while/body/eval_jaxpr/ppermute | solution.py:27
  230.1 9.6 %collective-permute-done = bf16[128,1024]{1,0:T(8,128)(2,1)S(1)} collective-permute-done((bf16[128,1024]{1,0:T(8,128)(2,1)}, bf16[128,1024]{1,0:T(8,128)(2,1)S(1)}, u32[]{:S(2)}, u32[]{:S(2)}) %collective-permute-start) | collective-permute-done | bytes 262176 | tf_op jit(solution)/shard_map/while/body/eval_jaxpr/ppermute | solution.py:27
  244.3 9.6 %collective-permute-done = bf16[128,1024]{1,0:T(8,128)(2,1)S(1)} collective-permute-done((bf16[128,1024]{1,0:T(8,128)(2,1)}, bf16[128,1024]{1,0:T(8,128)(2,1)S(1)}, u32[]{:S(2)}, u32[]{:S(2)}) %collective-permute-start) | collective-permute-done | bytes 262176 | tf_op jit(solution)/shard_map/while/body/eval_jaxpr/ppermute | solution.py:27
  258.4 9.6 %collective-permute-done = bf16[128,1024]{1,0:T(8,128)(2,1)S(1)} collective-permute-done((bf16[128,1024]{1,0:T(8,128)(2,1)}, bf16[128,1024]{1,0:T(8,128)(2,1)S(1)}, u32[]{:S(2)}, u32[]{:S(2)}) %collective-permute-start) | collective-permute-done | bytes 262176 | tf_op jit(solution)/shard_map/while/body/eval_jaxpr/ppermute | solution.py:27
  272.5 9.6 %collective-permute-done = bf16[128,1024]{1,0:T(8,128)(2,1)S(1)} collective-permute-done((bf16[128,1024]{1,0:T(8,128)(2,1)}, bf16[128,1024]{1,0:T(8,128)(2,1)S(1)}, u32[]{:S(2)}, u32[]{:S(2)}) %collective-permute-start) | collective-permute-done | bytes 262176 | tf_op jit(solution)/shard_map/while/body/eval_jaxpr/ppermute | solution.py:27
  286.6 9.6 %collective-permute-done = bf16[128,1024]{1,0:T(8,128)(2,1)S(1)} collective-permute-done((bf16[128,1024]{1,0:T(8,128)(2,1)}, bf16[128,1024]{1,0:T(8,128)(2,1)S(1)}, u32[]{:S(2)}, u32[]{:S(2)}) %collective-permute-start) | collective-permute-done | bytes 262176 | tf_op jit(solution)/shard_map/while/body/eval_jaxpr/ppermute | solution.py:27
  300.8 9.6 %collective-permute-done = bf16[128,1024]{1,0:T(8,128)(2,1)S(1)} collective-permute-done((bf16[128,1024]{1,0:T(8,128)(2,1)}, bf16[128,1024]{1,0:T(8,128)(2,1)S(1)}, u32[]{:S(2)}, u32[]{:S(2)}) %collective-permute-start) | collective-permute-done | bytes 262176 | tf_op jit(solution)/shard_map/while/body/eval_jaxpr/ppermute | solution.py:27
  314.9 9.6 %collective-permute-done = bf16[128,1024]{1,0:T(8,128)(2,1)S(1)} collective-permute-done((bf16[128,1024]{1,0:T(8,128)(2,1)}, bf16[128,1024]{1,0:T(8,128)(2,1)S(1)}, u32[]{:S(2)}, u32[]{:S(2)}) %collective-permute-start) | collective-permute-done | bytes 262176 | tf_op jit(solution)/shard_map/while/body/eval_jaxpr/ppermute | solution.py:27
  329.0 9.6 %collective-permute-done = bf16[128,1024]{1,0:T(8,128)(2,1)S(1)} collective-permute-done((bf16[128,1024]{1,0:T(8,128)(2,1)}, bf16[128,1024]{1,0:T(8,128)(2,1)S(1)}, u32[]{:S(2)}, u32[]{:S(2)}) %collective-permute-start) | collective-permute-done | bytes 262176 | tf_op jit(solution)/shard_map/while/body/eval_jaxpr/ppermute | solution.py:27
  343.1 9.6 %collective-permute-done = bf16[128,1024]{1,0:T(8,128)(2,1)S(1)} collective-permute-done((bf16[128,1024]{1,0:T(8,128)(2,1)}, bf16[128,1024]{1,0:T(8,128)(2,1)S(1)}, u32[]{:S(2)}, u32[]{:S(2)}) %collective-permute-start) | collective-permute-done | bytes 262176 | tf_op jit(solution)/shard_map/while/body/eval_jaxpr/ppermute | solution.py:27
  (177 shorter events, 100.1 us)
Async XLA Ops:
  7.2 89.8 %copy-start = (bf16[512,1024]{1,0:T(8,128)(2,1)S(1)}, bf16[512,1024]{1,0:T(8,128)(2,1)}, u32[]{:S(2)}) copy-start(bf16[512,1024]{1,0:T(8,128)(2,1)} %param.17) | copy-start | bytes 3145732
  7.2 81.0 %all-gather.2.cloned.1.call-start = ((), (), s32[]{:S(2)}) async-start(), calls=%async_computation | async-start | bytes 4456448 | tf_op jit(solution)/shard_map/all_gather | solution.py:107
  13.0 18.0 %collective-permute-start.2 = (bf16[128,1024]{1,0:T(8,128)(2,1)}, bf16[128,1024]{1,0:T(8,128)(2,1)S(1)}, u32[]{:S(2)}, u32[]{:S(2)}) collective-permute-start(bf16[128,1024]{1,0:T(8,128)(2,1)} %pad_maximum_fusion.2), channel_id=1, source_target_pairs={{1,0},{2,1},{3,2},{4,3},{5,4},{6,5},{7,6},{8,7},{9,8},{10,9},{11,1... | collective-permute-start | bytes 786440 | tf_op jit(solution)/shard_map/ppermute | solution.py:20
  24.3 12.0 %collective-permute-start.1 = (bf16[128,1024]{1,0:T(8,128)(2,1)}, bf16[128,1024]{1,0:T(8,128)(2,1)S(1)}, u32[]{:S(2)}, u32[]{:S(2)}) collective-permute-start(bf16[128,1024]{1,0:T(8,128)(2,1)} %pad_maximum_fusion.2), channel_id=1, source_target_pairs={{0,1},{1,2},{2,3},{3,4},{4,5},{5,6},{6,7},{7,8},{8,9},{9,10},{10,1... | collective-permute-start | bytes 786440 | tf_op jit(solution)/shard_map/ppermute | solution.py:19
  94.8 3.3 copy-start.26
  95.8 3.3 copy-start.16
  96.2 7.2 %copy-start.7 = (f32[128,512]{1,0:T(8,128)}, f32[128,512]{1,0:T(8,128)S(1)}, u32[]{:S(2)}) copy-start(f32[128,512]{1,0:T(8,128)S(1)} %get-tuple-element.134) | copy-start | bytes 786436
  111.2 2.5 copy-start.2
  122.3 2.5 copy-start.25
  131.1 11.6 %copy-start.4 = (f32[16,128,1024]{2,1,0:T(8,128)}, f32[16,128,1024]{2,1,0:T(8,128)S(1)}, u32[]{:S(2)}) copy-start(f32[16,128,1024]{2,1,0:T(8,128)S(1)} %copy.29) | copy-start | bytes 25165828
  133.9 220.7 %collective-permute-start.4 = (bf16[128,1024]{1,0:T(8,128)(2,1)}, bf16[128,1024]{1,0:T(8,128)(2,1)}, u32[]{:S(2)}, u32[]{:S(2)}) collective-permute-start(bf16[128,1024]{1,0:T(8,128)(2,1)} %get-tuple-element.128), channel_id=1, source_target_pairs={{0,1},{1,2},{2,3},{3,4},{4,5},{5,6},{6,7},{7,8},{8,9},{9,10},{10,1... | collective-permute-start | bytes 786440 | tf_op jit(solution)/shard_map/ppermute | solution.py:27
  137.3 217.3 %collective-permute-start.3 = (bf16[128,1024]{1,0:T(8,128)(2,1)}, bf16[128,1024]{1,0:T(8,128)(2,1)}, u32[]{:S(2)}, u32[]{:S(2)}) collective-permute-start(bf16[128,1024]{1,0:T(8,128)(2,1)} %get-tuple-element.127), channel_id=1, source_target_pairs={{0,31},{1,0},{2,1},{3,2},{4,3},{5,4},{6,5},{7,6},{8,7},{9,8},{10,9... | collective-permute-start | bytes 786440 | tf_op jit(solution)/shard_map/ppermute | solution.py:27
  143.4 11.5 %collective-permute-start = (bf16[128,1024]{1,0:T(8,128)(2,1)}, bf16[128,1024]{1,0:T(8,128)(2,1)S(1)}, u32[]{:S(2)}, u32[]{:S(2)}) collective-permute-start(bf16[128,1024]{1,0:T(8,128)(2,1)} %convert_element_type.201), channel_id=1, source_target_pairs={{0,32},{32,64},{64,96},{96,128},{128,160},{160,192},{192,224},{224... | collective-permute-start | bytes 786440 | tf_op jit(solution)/shard_map/while/body/eval_jaxpr/ppermute | solution.py:27
  157.6 11.5 %collective-permute-start = (bf16[128,1024]{1,0:T(8,128)(2,1)}, bf16[128,1024]{1,0:T(8,128)(2,1)S(1)}, u32[]{:S(2)}, u32[]{:S(2)}) collective-permute-start(bf16[128,1024]{1,0:T(8,128)(2,1)} %convert_element_type.201), channel_id=1, source_target_pairs={{0,32},{32,64},{64,96},{96,128},{128,160},{160,192},{192,224},{224... | collective-permute-start | bytes 786440 | tf_op jit(solution)/shard_map/while/body/eval_jaxpr/ppermute | solution.py:27
  171.7 11.5 %collective-permute-start = (bf16[128,1024]{1,0:T(8,128)(2,1)}, bf16[128,1024]{1,0:T(8,128)(2,1)S(1)}, u32[]{:S(2)}, u32[]{:S(2)}) collective-permute-start(bf16[128,1024]{1,0:T(8,128)(2,1)} %convert_element_type.201), channel_id=1, source_target_pairs={{0,32},{32,64},{64,96},{96,128},{128,160},{160,192},{192,224},{224... | collective-permute-start | bytes 786440 | tf_op jit(solution)/shard_map/while/body/eval_jaxpr/ppermute | solution.py:27
  185.8 11.5 %collective-permute-start = (bf16[128,1024]{1,0:T(8,128)(2,1)}, bf16[128,1024]{1,0:T(8,128)(2,1)S(1)}, u32[]{:S(2)}, u32[]{:S(2)}) collective-permute-start(bf16[128,1024]{1,0:T(8,128)(2,1)} %convert_element_type.201), channel_id=1, source_target_pairs={{0,32},{32,64},{64,96},{96,128},{128,160},{160,192},{192,224},{224... | collective-permute-start | bytes 786440 | tf_op jit(solution)/shard_map/while/body/eval_jaxpr/ppermute | solution.py:27
  199.9 11.5 %collective-permute-start = (bf16[128,1024]{1,0:T(8,128)(2,1)}, bf16[128,1024]{1,0:T(8,128)(2,1)S(1)}, u32[]{:S(2)}, u32[]{:S(2)}) collective-permute-start(bf16[128,1024]{1,0:T(8,128)(2,1)} %convert_element_type.201), channel_id=1, source_target_pairs={{0,32},{32,64},{64,96},{96,128},{128,160},{160,192},{192,224},{224... | collective-permute-start | bytes 786440 | tf_op jit(solution)/shard_map/while/body/eval_jaxpr/ppermute | solution.py:27
  214.1 11.5 %collective-permute-start = (bf16[128,1024]{1,0:T(8,128)(2,1)}, bf16[128,1024]{1,0:T(8,128)(2,1)S(1)}, u32[]{:S(2)}, u32[]{:S(2)}) collective-permute-start(bf16[128,1024]{1,0:T(8,128)(2,1)} %convert_element_type.201), channel_id=1, source_target_pairs={{0,32},{32,64},{64,96},{96,128},{128,160},{160,192},{192,224},{224... | collective-permute-start | bytes 786440 | tf_op jit(solution)/shard_map/while/body/eval_jaxpr/ppermute | solution.py:27
  228.2 11.5 %collective-permute-start = (bf16[128,1024]{1,0:T(8,128)(2,1)}, bf16[128,1024]{1,0:T(8,128)(2,1)S(1)}, u32[]{:S(2)}, u32[]{:S(2)}) collective-permute-start(bf16[128,1024]{1,0:T(8,128)(2,1)} %convert_element_type.201), channel_id=1, source_target_pairs={{0,32},{32,64},{64,96},{96,128},{128,160},{160,192},{192,224},{224... | collective-permute-start | bytes 786440 | tf_op jit(solution)/shard_map/while/body/eval_jaxpr/ppermute | solution.py:27
  242.3 11.5 %collective-permute-start = (bf16[128,1024]{1,0:T(8,128)(2,1)}, bf16[128,1024]{1,0:T(8,128)(2,1)S(1)}, u32[]{:S(2)}, u32[]{:S(2)}) collective-permute-start(bf16[128,1024]{1,0:T(8,128)(2,1)} %convert_element_type.201), channel_id=1, source_target_pairs={{0,32},{32,64},{64,96},{96,128},{128,160},{160,192},{192,224},{224... | collective-permute-start | bytes 786440 | tf_op jit(solution)/shard_map/while/body/eval_jaxpr/ppermute | solution.py:27
  256.4 11.5 %collective-permute-start = (bf16[128,1024]{1,0:T(8,128)(2,1)}, bf16[128,1024]{1,0:T(8,128)(2,1)S(1)}, u32[]{:S(2)}, u32[]{:S(2)}) collective-permute-start(bf16[128,1024]{1,0:T(8,128)(2,1)} %convert_element_type.201), channel_id=1, source_target_pairs={{0,32},{32,64},{64,96},{96,128},{128,160},{160,192},{192,224},{224... | collective-permute-start | bytes 786440 | tf_op jit(solution)/shard_map/while/body/eval_jaxpr/ppermute | solution.py:27
  270.6 11.5 %collective-permute-start = (bf16[128,1024]{1,0:T(8,128)(2,1)}, bf16[128,1024]{1,0:T(8,128)(2,1)S(1)}, u32[]{:S(2)}, u32[]{:S(2)}) collective-permute-start(bf16[128,1024]{1,0:T(8,128)(2,1)} %convert_element_type.201), channel_id=1, source_target_pairs={{0,32},{32,64},{64,96},{96,128},{128,160},{160,192},{192,224},{224... | collective-permute-start | bytes 786440 | tf_op jit(solution)/shard_map/while/body/eval_jaxpr/ppermute | solution.py:27
  284.7 11.5 %collective-permute-start = (bf16[128,1024]{1,0:T(8,128)(2,1)}, bf16[128,1024]{1,0:T(8,128)(2,1)S(1)}, u32[]{:S(2)}, u32[]{:S(2)}) collective-permute-start(bf16[128,1024]{1,0:T(8,128)(2,1)} %convert_element_type.201), channel_id=1, source_target_pairs={{0,32},{32,64},{64,96},{96,128},{128,160},{160,192},{192,224},{224... | collective-permute-start | bytes 786440 | tf_op jit(solution)/shard_map/while/body/eval_jaxpr/ppermute | solution.py:27
  298.8 11.5 %collective-permute-start = (bf16[128,1024]{1,0:T(8,128)(2,1)}, bf16[128,1024]{1,0:T(8,128)(2,1)S(1)}, u32[]{:S(2)}, u32[]{:S(2)}) collective-permute-start(bf16[128,1024]{1,0:T(8,128)(2,1)} %convert_element_type.201), channel_id=1, source_target_pairs={{0,32},{32,64},{64,96},{96,128},{128,160},{160,192},{192,224},{224... | collective-permute-start | bytes 786440 | tf_op jit(solution)/shard_map/while/body/eval_jaxpr/ppermute | solution.py:27
  312.9 11.5 %collective-permute-start = (bf16[128,1024]{1,0:T(8,128)(2,1)}, bf16[128,1024]{1,0:T(8,128)(2,1)S(1)}, u32[]{:S(2)}, u32[]{:S(2)}) collective-permute-start(bf16[128,1024]{1,0:T(8,128)(2,1)} %convert_element_type.201), channel_id=1, source_target_pairs={{0,32},{32,64},{64,96},{96,128},{128,160},{160,192},{192,224},{224... | collective-permute-start | bytes 786440 | tf_op jit(solution)/shard_map/while/body/eval_jaxpr/ppermute | solution.py:27
  327.1 11.5 %collective-permute-start = (bf16[128,1024]{1,0:T(8,128)(2,1)}, bf16[128,1024]{1,0:T(8,128)(2,1)S(1)}, u32[]{:S(2)}, u32[]{:S(2)}) collective-permute-start(bf16[128,1024]{1,0:T(8,128)(2,1)} %convert_element_type.201), channel_id=1, source_target_pairs={{0,32},{32,64},{64,96},{96,128},{128,160},{160,192},{192,224},{224... | collective-permute-start | bytes 786440 | tf_op jit(solution)/shard_map/while/body/eval_jaxpr/ppermute | solution.py:27
  341.2 11.5 %collective-permute-start = (bf16[128,1024]{1,0:T(8,128)(2,1)}, bf16[128,1024]{1,0:T(8,128)(2,1)S(1)}, u32[]{:S(2)}, u32[]{:S(2)}) collective-permute-start(bf16[128,1024]{1,0:T(8,128)(2,1)} %convert_element_type.201), channel_id=1, source_target_pairs={{0,32},{32,64},{64,96},{96,128},{128,160},{160,192},{192,224},{224... | collective-permute-start | bytes 786440 | tf_op jit(solution)/shard_map/while/body/eval_jaxpr/ppermute | solution.py:27
  354.6 2.2 copy-start.8
  354.6 2.2 copy-start.13
  354.6 2.2 copy-start.17
  354.7 2.2 copy-start.20
  354.7 2.2 copy-start.22
  (29 other events, 29.3 us)
Sparse Core Ops, SparseCore 0:
  13.1 75.0 all-gather.1
where the time goes:
time: 366 us; the launch traced here: 365 us
  waiting for transfers between devices  199 us (54%)
  starting transfers between devices  50.6 us (14%)
  other arithmetic  41.9 us (11%)
  local copies, waits for them, and re-layouts  33.2 us (9%)
  matrix products  24.4 us (7%)
  between operations  14.6 us (4%)
    ppermute x17, waiting for transfers between devices, shifted(): lax.ppermute(array, axis, [(i, (i + by) % devices) for i in range(devices)])  143 us
    all_gather x1, waiting for transfers between devices, on_device(): panels = lax.all_gather(keyvals, 'blk', axis=0, tiled=True)  51.1 us
    ppermute x17, starting transfers between devices, shifted(): lax.ppermute(array, axis, [(i, (i + by) % devices) for i in range(devices)])  37.4 us
    add x15, other arithmetic, carry_step(): return running + lax.dynamic_slice_in_dim(far_parts, target * rows, rows, 0)  17.4 us
    ppermute x1, starting transfers between devices, with_halo(): after = lax.ppermute(leading, axis, down)  11.3 us
    convert_element_type x15, other arithmetic, carry_step(): running.astype(jnp.bfloat16)  11.1 us
    while x30, local copies, waits for them, and re-layouts  10.5 us
  transfers between devices with their start and end apart: 20, of which 17 were waited for; matrix products, arithmetic and copies ran while one was open for 10% of the time, Pallas kernels for 0%

commit v1 on v0

--- a/solution.py
+++ b/solution.py
@@ -104,7 +104,10 @@
     values = jnp.dot(normed, w_value, preferred_element_type=f32).astype(bf16)
     keyvals = jnp.concatenate([keys, values], 1)
     window = with_halo(keyvals, (("dom", 0),), rows)
-    panels = lax.all_gather(keyvals, "blk", axis=0, tiled=True)
+    size = lax.axis_size("blk")
+    shards = jnp.stack([keyvals for _ in range(size)])
+    shards = lax.all_to_all(shards, "blk", split_axis=0, concat_axis=0)
+    panels = jnp.concatenate(shards, axis=0)
     listed = experts_list[0]
     listed_count = listed.shape[0]
     chosen = jnp.take(panels.reshape(groups, rows, 2 * width), listed, axis=0)

time: 366 us -> 352 us (0.962)
  the two profiles are of different devices: /device:TPU:8 before, /device:TPU:16 now
where the time goes in v1:
time: 352 us; the launch traced here: 350 us
  waiting for transfers between devices  187 us (53%)
  starting transfers between devices  64.9 us (18%)
  other arithmetic  38.8 us (11%)
  local copies, waits for them, and re-layouts  34 us (10%)
  matrix products  24 us (7%)
    ppermute x17, waiting for transfers between devices, shifted(): lax.ppermute(array, axis, [(i, (i + by) % devices) for i in range(devices)])  143 us
    ppermute x17, starting transfers between devices, shifted(): lax.ppermute(array, axis, [(i, (i + by) % devices) for i in range(devices)])  43.4 us
    all_to_all x1, waiting for transfers between devices, on_device(): shards = lax.all_to_all(shards, 'blk', split_axis=0, concat_axis=0)  32.8 us
    add x15, other arithmetic, carry_step(): return running + lax.dynamic_slice_in_dim(far_parts, target * rows, rows, 0)  17.4 us
    convert_element_type x15, other arithmetic, carry_step(): running.astype(jnp.bfloat16)  11.2 us
    while x30, local copies, waits for them, and re-layouts  10.6 us
    all_to_all x1, starting transfers between devices, on_device(): shards = lax.all_to_all(shards, 'blk', split_axis=0, concat_axis=0)  10.1 us
    ppermute x1, starting transfers between devices, with_halo(): after = lax.ppermute(leading, axis, down)  9.39 us
  transfers between devices with their start and end apart: 20, of which 18 were waited for; matrix products, arithmetic and copies ran while one was open for 9% of the time, Pallas kernels for 0%

profile of v1, /device:TPU:16, one launch (start us, length us, event | category | flops | bytes accessed | tf_op | source)
XLA Modules:
  0.0 350.3 jit_solution(2719347351431978958)
XLA Ops:
  5.7 2.5 stack.2
  8.2 10.1 %all-to-all-start = ((bf16[16,128,1024]{2,1,0:T(8,128)(2,1)}), bf16[16,128,1024]{2,1,0:T(8,128)(2,1)}, u32[]{:S(2)}, u32[]{:S(2)}) async-start(bf16[16,128,1024]{2,1,0:T(8,128)(2,1)} %stack.2), calls=%async_computation | async-start | bytes 8388608 | tf_op jit(solution)/shard_map/all_to_all | solution.py:109
  18.3 9.4 %collective-permute-start.2 = (bf16[128,1024]{1,0:T(8,128)(2,1)S(1)}, bf16[128,1024]{1,0:T(8,128)(2,1)S(1)}, u32[]{:S(2)}, u32[]{:S(2)}) collective-permute-start(bf16[128,1024]{1,0:T(8,128)(2,1)S(1)} %pad_maximum_fusion.2), channel_id=1, source_target_pairs={{1,0},{2,1},{3,2},{4,3},{5,4},{6,5},{7,6},{8,7},{9,8},{10,9},{11,1... | collective-permute-start | bytes 786440 | tf_op jit(solution)/shard_map/ppermute | solution.py:20
  27.7 1.9 collective-permute-start.1
  31.1 7.0 %collective-permute-done.2 = bf16[128,1024]{1,0:T(8,128)(2,1)S(1)} collective-permute-done((bf16[128,1024]{1,0:T(8,128)(2,1)S(1)}, bf16[128,1024]{1,0:T(8,128)(2,1)S(1)}, u32[]{:S(2)}, u32[]{:S(2)}) %collective-permute-start.2) | collective-permute-done | bytes 262176 | tf_op jit(solution)/shard_map/ppermute | solution.py:20
  38.9 3.4 collective-permute-done.1
  43.2 32.8 %all-to-all-done = bf16[16,128,1024]{2,1,0:T(8,128)(2,1)} async-done(((bf16[16,128,1024]{2,1,0:T(8,128)(2,1)}), bf16[16,128,1024]{2,1,0:T(8,128)(2,1)}, u32[]{:S(2)}, u32[]{:S(2)}) %all-to-all-start) | async-done | bytes 4194336 | tf_op jit(solution)/shard_map/all_to_all | solution.py:109
  76.0 2.8 gather_fusion
  86.9 3.7 %fusion.82 = (f32[128]{0:T(128)}, f32[128]{0:T(128)}, f32[128,512]{1,0:T(8,128)}) fusion(f32[128]{0:T(128)} %copy-done.21, f32[128,512]{1,0:T(8,128)S(1)} %get-tuple-element.134, f32[128]{0:T(128)S(1)} %broadcast_multiply_fusion.4, bf16[512,1024]{1,0:T(8,128)(2,1)S(1)} %copy-done, f32[128,1024]{1,0:T(8,128)} %copy-done.16, ...), kind=kOutput, calls=%fused_computation.117 | convolution fusion | flops 271384320 | bytes 3278848 | tf_op jit(solution)/shard_map/dot_general | solution.py:124
  91.8 2.1 convolution_convert_fusion.1
  95.9 3.3 multiply_convert_fusion
  102.4 2.1 fusion.7
  106.3 2.8 copy.26
  114.4 4.9 %copy.28 = f32[16,128,1024]{2,1,0:T(8,128)S(1)} copy(f32[16,128,1024]{2,0,1:T(8,128)S(1)} %fusion.5) | data formatting | bytes 16777216 | tf_op jit(solution)/shard_map/eg,erc->grc/dot_general | solution.py:137
  122.1 12.8 %collective-permute-start.3 = (bf16[128,1024]{1,0:T(8,128)(2,1)}, bf16[128,1024]{1,0:T(8,128)(2,1)}, u32[]{:S(2)}, u32[]{:S(2)}) collective-permute-start(bf16[128,1024]{1,0:T(8,128)(2,1)} %get-tuple-element.127), channel_id=1, source_target_pairs={{0,31},{1,0},{2,1},{3,2},{4,3},{5,4},{6,5},{7,6},{8,7},{9,8},{10,9... | collective-permute-start | bytes 786440 | tf_op jit(solution)/shard_map/ppermute | solution.py:27
  135.0 212.1 %while.15 = (s32[]{:T(128)}, f32[128,1024]{1,0:T(8,128)S(1)}, s32[]{:T(128)}, f32[2048,1024]{1,0:T(8,128)}, s32[]{:T(128)}, /*index=5*/s32[]{:T(128)}, s32[]{:T(...) while((s32[]{:T(128)}, f32[128,1024]{1,0:T(8,128)S(1)}, s32[]{:T(128)}, f32[2048,1024]{1,0:T(8,128)}, ...), condition=%wide.region_10.11_spmd, body=%wide.region_9.10_spmd.sunk | while | flops 393235 | bytes 4194664 | solution.py:145
  135.7 2.0 collective-permute-start
  137.8 9.5 %collective-permute-done = bf16[128,1024]{1,0:T(8,128)(2,1)S(1)} collective-permute-done((bf16[128,1024]{1,0:T(8,128)(2,1)}, bf16[128,1024]{1,0:T(8,128)(2,1)S(1)}, u32[]{:S(2)}, u32[]{:S(2)}) %collective-permute-start) | collective-permute-done | bytes 262176 | tf_op jit(solution)/shard_map/while/body/eval_jaxpr/ppermute | solution.py:27
  151.8 9.6 %collective-permute-done = bf16[128,1024]{1,0:T(8,128)(2,1)S(1)} collective-permute-done((bf16[128,1024]{1,0:T(8,128)(2,1)}, bf16[128,1024]{1,0:T(8,128)(2,1)S(1)}, u32[]{:S(2)}, u32[]{:S(2)}) %collective-permute-start) | collective-permute-done | bytes 262176 | tf_op jit(solution)/shard_map/while/body/eval_jaxpr/ppermute | solution.py:27
  166.0 9.6 %collective-permute-done = bf16[128,1024]{1,0:T(8,128)(2,1)S(1)} collective-permute-done((bf16[128,1024]{1,0:T(8,128)(2,1)}, bf16[128,1024]{1,0:T(8,128)(2,1)S(1)}, u32[]{:S(2)}, u32[]{:S(2)}) %collective-permute-start) | collective-permute-done | bytes 262176 | tf_op jit(solution)/shard_map/while/body/eval_jaxpr/ppermute | solution.py:27
  180.1 9.6 %collective-permute-done = bf16[128,1024]{1,0:T(8,128)(2,1)S(1)} collective-permute-done((bf16[128,1024]{1,0:T(8,128)(2,1)}, bf16[128,1024]{1,0:T(8,128)(2,1)S(1)}, u32[]{:S(2)}, u32[]{:S(2)}) %collective-permute-start) | collective-permute-done | bytes 262176 | tf_op jit(solution)/shard_map/while/body/eval_jaxpr/ppermute | solution.py:27
  194.2 9.6 %collective-permute-done = bf16[128,1024]{1,0:T(8,128)(2,1)S(1)} collective-permute-done((bf16[128,1024]{1,0:T(8,128)(2,1)}, bf16[128,1024]{1,0:T(8,128)(2,1)S(1)}, u32[]{:S(2)}, u32[]{:S(2)}) %collective-permute-start) | collective-permute-done | bytes 262176 | tf_op jit(solution)/shard_map/while/body/eval_jaxpr/ppermute | solution.py:27
  208.4 9.6 %collective-permute-done = bf16[128,1024]{1,0:T(8,128)(2,1)S(1)} collective-permute-done((bf16[128,1024]{1,0:T(8,128)(2,1)}, bf16[128,1024]{1,0:T(8,128)(2,1)S(1)}, u32[]{:S(2)}, u32[]{:S(2)}) %collective-permute-start) | collective-permute-done | bytes 262176 | tf_op jit(solution)/shard_map/while/body/eval_jaxpr/ppermute | solution.py:27
  222.5 9.6 %collective-permute-done = bf16[128,1024]{1,0:T(8,128)(2,1)S(1)} collective-permute-done((bf16[128,1024]{1,0:T(8,128)(2,1)}, bf16[128,1024]{1,0:T(8,128)(2,1)S(1)}, u32[]{:S(2)}, u32[]{:S(2)}) %collective-permute-start) | collective-permute-done | bytes 262176 | tf_op jit(solution)/shard_map/while/body/eval_jaxpr/ppermute | solution.py:27
  236.7 9.6 %collective-permute-done = bf16[128,1024]{1,0:T(8,128)(2,1)S(1)} collective-permute-done((bf16[128,1024]{1,0:T(8,128)(2,1)}, bf16[128,1024]{1,0:T(8,128)(2,1)S(1)}, u32[]{:S(2)}, u32[]{:S(2)}) %collective-permute-start) | collective-permute-done | bytes 262176 | tf_op jit(solution)/shard_map/while/body/eval_jaxpr/ppermute | solution.py:27
  250.8 9.6 %collective-permute-done = bf16[128,1024]{1,0:T(8,128)(2,1)S(1)} collective-permute-done((bf16[128,1024]{1,0:T(8,128)(2,1)}, bf16[128,1024]{1,0:T(8,128)(2,1)S(1)}, u32[]{:S(2)}, u32[]{:S(2)}) %collective-permute-start) | collective-permute-done | bytes 262176 | tf_op jit(solution)/shard_map/while/body/eval_jaxpr/ppermute | solution.py:27
  264.9 9.6 %collective-permute-done = bf16[128,1024]{1,0:T(8,128)(2,1)S(1)} collective-permute-done((bf16[128,1024]{1,0:T(8,128)(2,1)}, bf16[128,1024]{1,0:T(8,128)(2,1)S(1)}, u32[]{:S(2)}, u32[]{:S(2)}) %collective-permute-start) | collective-permute-done | bytes 262176 | tf_op jit(solution)/shard_map/while/body/eval_jaxpr/ppermute | solution.py:27
  279.1 9.6 %collective-permute-done = bf16[128,1024]{1,0:T(8,128)(2,1)S(1)} collective-permute-done((bf16[128,1024]{1,0:T(8,128)(2,1)}, bf16[128,1024]{1,0:T(8,128)(2,1)S(1)}, u32[]{:S(2)}, u32[]{:S(2)}) %collective-permute-start) | collective-permute-done | bytes 262176 | tf_op jit(solution)/shard_map/while/body/eval_jaxpr/ppermute | solution.py:27
  293.2 9.6 %collective-permute-done = bf16[128,1024]{1,0:T(8,128)(2,1)S(1)} collective-permute-done((bf16[128,1024]{1,0:T(8,128)(2,1)}, bf16[128,1024]{1,0:T(8,128)(2,1)S(1)}, u32[]{:S(2)}, u32[]{:S(2)}) %collective-permute-start) | collective-permute-done | bytes 262176 | tf_op jit(solution)/shard_map/while/body/eval_jaxpr/ppermute | solution.py:27
  307.4 9.6 %collective-permute-done = bf16[128,1024]{1,0:T(8,128)(2,1)S(1)} collective-permute-done((bf16[128,1024]{1,0:T(8,128)(2,1)}, bf16[128,1024]{1,0:T(8,128)(2,1)S(1)}, u32[]{:S(2)}, u32[]{:S(2)}) %collective-permute-start) | collective-permute-done | bytes 262176 | tf_op jit(solution)/shard_map/while/body/eval_jaxpr/ppermute | solution.py:27
  321.5 9.6 %collective-permute-done = bf16[128,1024]{1,0:T(8,128)(2,1)S(1)} collective-permute-done((bf16[128,1024]{1,0:T(8,128)(2,1)}, bf16[128,1024]{1,0:T(8,128)(2,1)S(1)}, u32[]{:S(2)}, u32[]{:S(2)}) %collective-permute-start) | collective-permute-done | bytes 262176 | tf_op jit(solution)/shard_map/while/body/eval_jaxpr/ppermute | solution.py:27
  335.6 9.6 %collective-permute-done = bf16[128,1024]{1,0:T(8,128)(2,1)S(1)} collective-permute-done((bf16[128,1024]{1,0:T(8,128)(2,1)}, bf16[128,1024]{1,0:T(8,128)(2,1)S(1)}, u32[]{:S(2)}, u32[]{:S(2)}) %collective-permute-start) | collective-permute-done | bytes 262176 | tf_op jit(solution)/shard_map/while/body/eval_jaxpr/ppermute | solution.py:27
  (183 shorter events, 101.3 us)
Async XLA Ops:
  0.6 84.1 %copy-start = (bf16[512,1024]{1,0:T(8,128)(2,1)S(1)}, bf16[512,1024]{1,0:T(8,128)(2,1)}, u32[]{:S(2)}) copy-start(bf16[512,1024]{1,0:T(8,128)(2,1)} %param.17) | copy-start | bytes 3145732
  8.2 21.5 %copy-start.27 = (s32[1,4]{1,0:T(1,128)S(1)}, s32[1,4]{1,0:T(1,128)}, u32[]{:S(2)}) copy-start(s32[1,4]{1,0:T(1,128)} %param.12) | copy-start | bytes 52
  8.2 21.5 %copy-start.5 = (bf16[128,512]{1,0:T(8,128)(2,1)S(1)}, bf16[128,512]{1,0:T(8,128)(2,1)}, u32[]{:S(2)}) copy-start(bf16[128,512]{1,0:T(8,128)(2,1)} %param.11) | copy-start | bytes 393220
  8.2 21.5 %copy-start.9 = (bf16[512,512]{1,0:T(8,128)(2,1)S(1)}, bf16[512,512]{1,0:T(8,128)(2,1)}, u32[]{:S(2)}) copy-start(bf16[512,512]{1,0:T(8,128)(2,1)} %param.13) | copy-start | bytes 1572868
  8.2 67.9 %all-to-all-start = ((bf16[16,128,1024]{2,1,0:T(8,128)(2,1)}), bf16[16,128,1024]{2,1,0:T(8,128)(2,1)}, u32[]{:S(2)}, u32[]{:S(2)}) async-start(bf16[16,128,1024]{2,1,0:T(8,128)(2,1)} %stack.2), calls=%async_computation | async-start | bytes 8388608 | tf_op jit(solution)/shard_map/all_to_all | solution.py:109
  18.3 19.7 %collective-permute-start.2 = (bf16[128,1024]{1,0:T(8,128)(2,1)S(1)}, bf16[128,1024]{1,0:T(8,128)(2,1)S(1)}, u32[]{:S(2)}, u32[]{:S(2)}) collective-permute-start(bf16[128,1024]{1,0:T(8,128)(2,1)S(1)} %pad_maximum_fusion.2), channel_id=1, source_target_pairs={{1,0},{2,1},{3,2},{4,3},{5,4},{6,5},{7,6},{8,7},{9,8},{10,9},{11,1... | collective-permute-start | bytes 786440 | tf_op jit(solution)/shard_map/ppermute | solution.py:20
  27.7 14.6 %collective-permute-start.1 = (bf16[128,1024]{1,0:T(8,128)(2,1)S(1)}, bf16[128,1024]{1,0:T(8,128)(2,1)S(1)}, u32[]{:S(2)}, u32[]{:S(2)}) collective-permute-start(bf16[128,1024]{1,0:T(8,128)(2,1)S(1)} %pad_maximum_fusion.2), channel_id=1, source_target_pairs={{0,1},{1,2},{2,3},{3,4},{4,5},{5,6},{6,7},{7,8},{8,9},{9,10},{10,1... | collective-permute-start | bytes 786440 | tf_op jit(solution)/shard_map/ppermute | solution.py:19
  82.6 3.3 copy-start.29
  83.6 3.3 copy-start.17
  84.0 7.3 %copy-start.7 = (f32[128,512]{1,0:T(8,128)}, f32[128,512]{1,0:T(8,128)S(1)}, u32[]{:S(2)}) copy-start(f32[128,512]{1,0:T(8,128)S(1)} %get-tuple-element.134) | copy-start | bytes 786436
  99.2 3.2 copy-start.2
  119.3 15.7 %copy-start.4 = (f32[16,128,1024]{2,1,0:T(8,128)}, f32[16,128,1024]{2,1,0:T(8,128)S(1)}, u32[]{:S(2)}) copy-start(f32[16,128,1024]{2,1,0:T(8,128)S(1)} %copy.28) | copy-start | bytes 25165828
  120.2 226.9 %collective-permute-start.4 = (bf16[128,1024]{1,0:T(8,128)(2,1)}, bf16[128,1024]{1,0:T(8,128)(2,1)}, u32[]{:S(2)}, u32[]{:S(2)}) collective-permute-start(bf16[128,1024]{1,0:T(8,128)(2,1)} %get-tuple-element.128), channel_id=1, source_target_pairs={{0,1},{1,2},{2,3},{3,4},{4,5},{5,6},{6,7},{7,8},{8,9},{9,10},{10,1... | collective-permute-start | bytes 786440 | tf_op jit(solution)/shard_map/ppermute | solution.py:27
  122.1 225.0 %collective-permute-start.3 = (bf16[128,1024]{1,0:T(8,128)(2,1)}, bf16[128,1024]{1,0:T(8,128)(2,1)}, u32[]{:S(2)}, u32[]{:S(2)}) collective-permute-start(bf16[128,1024]{1,0:T(8,128)(2,1)} %get-tuple-element.127), channel_id=1, source_target_pairs={{0,31},{1,0},{2,1},{3,2},{4,3},{5,4},{6,5},{7,6},{8,7},{9,8},{10,9... | collective-permute-start | bytes 786440 | tf_op jit(solution)/shard_map/ppermute | solution.py:27
  135.7 11.5 %collective-permute-start = (bf16[128,1024]{1,0:T(8,128)(2,1)}, bf16[128,1024]{1,0:T(8,128)(2,1)S(1)}, u32[]{:S(2)}, u32[]{:S(2)}) collective-permute-start(bf16[128,1024]{1,0:T(8,128)(2,1)} %convert_element_type.201), channel_id=1, source_target_pairs={{0,32},{32,64},{64,96},{96,128},{128,160},{160,192},{192,224},{224... | collective-permute-start | bytes 786440 | tf_op jit(solution)/shard_map/while/body/eval_jaxpr/ppermute | solution.py:27
  149.9 11.5 %collective-permute-start = (bf16[128,1024]{1,0:T(8,128)(2,1)}, bf16[128,1024]{1,0:T(8,128)(2,1)S(1)}, u32[]{:S(2)}, u32[]{:S(2)}) collective-permute-start(bf16[128,1024]{1,0:T(8,128)(2,1)} %convert_element_type.201), channel_id=1, source_target_pairs={{0,32},{32,64},{64,96},{96,128},{128,160},{160,192},{192,224},{224... | collective-permute-start | bytes 786440 | tf_op jit(solution)/shard_map/while/body/eval_jaxpr/ppermute | solution.py:27
  164.0 11.5 %collective-permute-start = (bf16[128,1024]{1,0:T(8,128)(2,1)}, bf16[128,1024]{1,0:T(8,128)(2,1)S(1)}, u32[]{:S(2)}, u32[]{:S(2)}) collective-permute-start(bf16[128,1024]{1,0:T(8,128)(2,1)} %convert_element_type.201), channel_id=1, source_target_pairs={{0,32},{32,64},{64,96},{96,128},{128,160},{160,192},{192,224},{224... | collective-permute-start | bytes 786440 | tf_op jit(solution)/shard_map/while/body/eval_jaxpr/ppermute | solution.py:27
  178.2 11.5 %collective-permute-start = (bf16[128,1024]{1,0:T(8,128)(2,1)}, bf16[128,1024]{1,0:T(8,128)(2,1)S(1)}, u32[]{:S(2)}, u32[]{:S(2)}) collective-permute-start(bf16[128,1024]{1,0:T(8,128)(2,1)} %convert_element_type.201), channel_id=1, source_target_pairs={{0,32},{32,64},{64,96},{96,128},{128,160},{160,192},{192,224},{224... | collective-permute-start | bytes 786440 | tf_op jit(solution)/shard_map/while/body/eval_jaxpr/ppermute | solution.py:27
  192.3 11.5 %collective-permute-start = (bf16[128,1024]{1,0:T(8,128)(2,1)}, bf16[128,1024]{1,0:T(8,128)(2,1)S(1)}, u32[]{:S(2)}, u32[]{:S(2)}) collective-permute-start(bf16[128,1024]{1,0:T(8,128)(2,1)} %convert_element_type.201), channel_id=1, source_target_pairs={{0,32},{32,64},{64,96},{96,128},{128,160},{160,192},{192,224},{224... | collective-permute-start | bytes 786440 | tf_op jit(solution)/shard_map/while/body/eval_jaxpr/ppermute | solution.py:27
  206.4 11.5 %collective-permute-start = (bf16[128,1024]{1,0:T(8,128)(2,1)}, bf16[128,1024]{1,0:T(8,128)(2,1)S(1)}, u32[]{:S(2)}, u32[]{:S(2)}) collective-permute-start(bf16[128,1024]{1,0:T(8,128)(2,1)} %convert_element_type.201), channel_id=1, source_target_pairs={{0,32},{32,64},{64,96},{96,128},{128,160},{160,192},{192,224},{224... | collective-permute-start | bytes 786440 | tf_op jit(solution)/shard_map/while/body/eval_jaxpr/ppermute | solution.py:27
  220.6 11.5 %collective-permute-start = (bf16[128,1024]{1,0:T(8,128)(2,1)}, bf16[128,1024]{1,0:T(8,128)(2,1)S(1)}, u32[]{:S(2)}, u32[]{:S(2)}) collective-permute-start(bf16[128,1024]{1,0:T(8,128)(2,1)} %convert_element_type.201), channel_id=1, source_target_pairs={{0,32},{32,64},{64,96},{96,128},{128,160},{160,192},{192,224},{224... | collective-permute-start | bytes 786440 | tf_op jit(solution)/shard_map/while/body/eval_jaxpr/ppermute | solution.py:27
  234.7 11.5 %collective-permute-start = (bf16[128,1024]{1,0:T(8,128)(2,1)}, bf16[128,1024]{1,0:T(8,128)(2,1)S(1)}, u32[]{:S(2)}, u32[]{:S(2)}) collective-permute-start(bf16[128,1024]{1,0:T(8,128)(2,1)} %convert_element_type.201), channel_id=1, source_target_pairs={{0,32},{32,64},{64,96},{96,128},{128,160},{160,192},{192,224},{224... | collective-permute-start | bytes 786440 | tf_op jit(solution)/shard_map/while/body/eval_jaxpr/ppermute | solution.py:27
  248.9 11.5 %collective-permute-start = (bf16[128,1024]{1,0:T(8,128)(2,1)}, bf16[128,1024]{1,0:T(8,128)(2,1)S(1)}, u32[]{:S(2)}, u32[]{:S(2)}) collective-permute-start(bf16[128,1024]{1,0:T(8,128)(2,1)} %convert_element_type.201), channel_id=1, source_target_pairs={{0,32},{32,64},{64,96},{96,128},{128,160},{160,192},{192,224},{224... | collective-permute-start | bytes 786440 | tf_op jit(solution)/shard_map/while/body/eval_jaxpr/ppermute | solution.py:27
  263.0 11.5 %collective-permute-start = (bf16[128,1024]{1,0:T(8,128)(2,1)}, bf16[128,1024]{1,0:T(8,128)(2,1)S(1)}, u32[]{:S(2)}, u32[]{:S(2)}) collective-permute-start(bf16[128,1024]{1,0:T(8,128)(2,1)} %convert_element_type.201), channel_id=1, source_target_pairs={{0,32},{32,64},{64,96},{96,128},{128,160},{160,192},{192,224},{224... | collective-permute-start | bytes 786440 | tf_op jit(solution)/shard_map/while/body/eval_jaxpr/ppermute | solution.py:27
  277.1 11.5 %collective-permute-start = (bf16[128,1024]{1,0:T(8,128)(2,1)}, bf16[128,1024]{1,0:T(8,128)(2,1)S(1)}, u32[]{:S(2)}, u32[]{:S(2)}) collective-permute-start(bf16[128,1024]{1,0:T(8,128)(2,1)} %convert_element_type.201), channel_id=1, source_target_pairs={{0,32},{32,64},{64,96},{96,128},{128,160},{160,192},{192,224},{224... | collective-permute-start | bytes 786440 | tf_op jit(solution)/shard_map/while/body/eval_jaxpr/ppermute | solution.py:27
  291.3 11.5 %collective-permute-start = (bf16[128,1024]{1,0:T(8,128)(2,1)}, bf16[128,1024]{1,0:T(8,128)(2,1)S(1)}, u32[]{:S(2)}, u32[]{:S(2)}) collective-permute-start(bf16[128,1024]{1,0:T(8,128)(2,1)} %convert_element_type.201), channel_id=1, source_target_pairs={{0,32},{32,64},{64,96},{96,128},{128,160},{160,192},{192,224},{224... | collective-permute-start | bytes 786440 | tf_op jit(solution)/shard_map/while/body/eval_jaxpr/ppermute | solution.py:27
  305.4 11.5 %collective-permute-start = (bf16[128,1024]{1,0:T(8,128)(2,1)}, bf16[128,1024]{1,0:T(8,128)(2,1)S(1)}, u32[]{:S(2)}, u32[]{:S(2)}) collective-permute-start(bf16[128,1024]{1,0:T(8,128)(2,1)} %convert_element_type.201), channel_id=1, source_target_pairs={{0,32},{32,64},{64,96},{96,128},{128,160},{160,192},{192,224},{224... | collective-permute-start | bytes 786440 | tf_op jit(solution)/shard_map/while/body/eval_jaxpr/ppermute | solution.py:27
  319.6 11.5 %collective-permute-start = (bf16[128,1024]{1,0:T(8,128)(2,1)}, bf16[128,1024]{1,0:T(8,128)(2,1)S(1)}, u32[]{:S(2)}, u32[]{:S(2)}) collective-permute-start(bf16[128,1024]{1,0:T(8,128)(2,1)} %convert_element_type.201), channel_id=1, source_target_pairs={{0,32},{32,64},{64,96},{96,128},{128,160},{160,192},{192,224},{224... | collective-permute-start | bytes 786440 | tf_op jit(solution)/shard_map/while/body/eval_jaxpr/ppermute | solution.py:27
  333.7 11.5 %collective-permute-start = (bf16[128,1024]{1,0:T(8,128)(2,1)}, bf16[128,1024]{1,0:T(8,128)(2,1)S(1)}, u32[]{:S(2)}, u32[]{:S(2)}) collective-permute-start(bf16[128,1024]{1,0:T(8,128)(2,1)} %convert_element_type.201), channel_id=1, source_target_pairs={{0,32},{32,64},{64,96},{96,128},{128,160},{160,192},{192,224},{224... | collective-permute-start | bytes 786440 | tf_op jit(solution)/shard_map/while/body/eval_jaxpr/ppermute | solution.py:27
  347.1 2.2 copy-start.8
  347.1 2.2 copy-start.14
  347.2 2.2 copy-start.18
  (32 other events, 34.7 us)
